TPU v7x, 32 devices: a whole 2x2x4 slice. The times are simulated.
32 devices in a mesh: section: 4 (over y, x), vocab: 8 (over z, core), dp: 1.
Axes of the slice: x: 2, y: 2, z: 4, core: 2. Of those that a mesh axis runs over, the one named last changes fastest.
Arguments:
- hidden: bfloat16 [1, 512, 3072], P('dp', ('section', 'vocab')), may hold values from -160 to 160
- head: bfloat16 [131072, 3072], P(('section', 'vocab')), may hold values from -3 to 3
- labels: int32 [1, 512], P('dp'), may hold values from 0 to 131071
- response_mask: int32 [1, 512], P('dp'), may hold values from 0 to 1, as said below
- seq_pair: int32 [1, 4], P('dp'), may hold values from 0 to 3, as said below
- ref_logp: float32 [4], replicated, may hold values from -12.6 to -12.4
Outputs:
- token_logprob: float32 [1, 512], P('dp', ('section', 'vocab'))
- pair_margin: float32 [2], replicated
- loss: float32 [], replicated
Inputs may be any that keep to these rules, and one draw needn't show every extreme that they name: `response_mask`: each sequence of 128 rows has more than half of its rows set. `seq_pair`: over all replicas every slot of 0 to 3 appears once; slot q belongs to pair q // 2 and is its chosen response when q is even.
All inputs are finite; a program needn't handle non-finite values.
Results may differ from a plain program's by a relative error of at most 0.0003.
Values may be sent and summed in bfloat16 or wider, within the bound.
A program may use at most 64 MiB of HBM per device.

v0:
```python
import jax
import jax.numpy as jnp
from jax import lax
from jax.sharding import PartitionSpec as P

SEQ_DP = 4
beta_scale = 5.0


def body(hidden, head, labels, response_mask, seq_pair, ref_logp):
    shard_rows = hidden.shape[1]
    vocab_rows = head.shape[0]
    chip_rows = lax.all_gather(hidden, "vocab", axis=1, tiled=True)
    gathered = lax.all_gather(chip_rows, "section", axis=1, tiled=True)
    logits = lax.dot_general(
        gathered[0], head, (((1,), (1,)), ((), ())), preferred_element_type=jnp.float32
    )
    position = lax.axis_index(("section", "vocab"))
    local_max = jnp.max(logits, axis=1)
    local_sum = jnp.sum(jnp.exp(logits - local_max[:, None]), axis=1)
    target = labels[0] - position * vocab_rows
    column = lax.broadcasted_iota(jnp.int32, logits.shape, 1)
    label_part = jnp.sum(jnp.where(column == target[:, None], logits, 0.0), axis=1)
    whole_max = lax.pmax(local_max, ("section", "vocab"))
    total, label_logit = lax.psum(
        (local_sum * jnp.exp(local_max - whole_max), label_part), ("section", "vocab")
    )
    logprob = label_logit - whole_max - jnp.log(total)
    own_rows = lax.dynamic_slice_in_dim(logprob, position * shard_rows, shard_rows)
    token_logprob = own_rows[None, :]
    all_rows = logprob.shape[0]
    seq_len = all_rows // SEQ_DP
    slot_count = ref_logp.shape[0]
    weights = response_mask[0].astype(jnp.float32)
    counts = jnp.sum(weights.reshape(SEQ_DP, seq_len), axis=1)
    slot_ids = lax.broadcasted_iota(jnp.int32, (SEQ_DP, slot_count), 1)
    in_pair = (seq_pair[0][:, None] == slot_ids).astype(jnp.float32)
    seq_sums = jnp.sum((logprob * weights).reshape(SEQ_DP, seq_len), axis=1)
    seq_means = seq_sums / counts
    policy = lax.psum(jnp.sum(in_pair * seq_means[:, None], axis=0), "dp")
    pair_margin = beta_scale * (policy[0::2] - ref_logp[0::2] - (policy[1::2] - ref_logp[1::2]))
    loss = jnp.mean(jnp.logaddexp(0.0, -pair_margin))
    return (token_logprob, pair_margin, loss)


def solution(mesh):
    placed = (
        P("dp", ("section", "vocab"), None),
        P(("section", "vocab"), None),
        P("dp", None),
        P("dp", None),
        P("dp", None),
        P(),
    )
    return jax.shard_map(
        body,
        mesh=mesh,
        in_specs=placed,
        out_specs=(P("dp", ("section", "vocab")), P(), P()),
        check_vma=False,
    )
```

profile of v0, /device:TPU:0, one launch (start us, length us, event | category | flops | bytes accessed | tf_op | source)
XLA Modules:
  0.0 187.5 jit_solution(17460948723642342068)
XLA Ops:
  7.2 0.0 all-gather.2.cloned.1.call-start
  7.2 18.5 %all_gather.6 = bf16[1,128,3072]{2,1,0:T(8,128)(2,1)} all-gather(bf16[1,16,3072]{2,1,0:T(8,128)(2,1)} %param.6), channel_id=1, replica_groups=mesh['section'=4,'vocab'=8,'dp'=1] {'vocab'}, dimensions={1}, use_global_device_ids=true | all-gather | bytes 884736 | tf_op jit(solution)/shard_map/all_gather | solution.py:13
  25.7 0.0 all-gather.2.cloned.1.call-update
  25.8 0.7 slice.13
  26.5 0.7 slice.15
  27.2 0.7 convert_element_type.15
  27.9 0.1 reduce_sum.57
  28.0 0.7 broadcast_subtract_fusion
  28.7 41.9 %all-gather.2.cloned.1.call-done = bf16[1,512,3072]{2,1,0:T(8,128)(2,1)} async-done(((bf16[1,128,3072]{2,1,0:T(8,128)(2,1)}), bf16[1,512,3072]{2,1,0:T(8,128)(2,1)}) %all-gather.2.cloned.1.call-update) | async-done | bytes 3145744 | tf_op jit(solution)/shard_map/all_gather | solution.py:14
  70.6 21.0 %fusion.3 = (f32[512]{0:T(512)S(1)}, f32[512,4096]{1,0:T(8,128)}) fusion(bf16[4096,3072]{1,0:T(8,128)(2,1)} %param.7, bf16[1,512,3072]{2,1,0:T(8,128)(2,1)} %all-gather.2.cloned.1.call-done), kind=kOutput, calls=%fused_computation.15 | convolution fusion | flops 12886999040 | bytes 36702208 | tf_op jit(solution)/shard_map/dot_general | solution.py:15
  91.6 0.0 copy-start
  91.6 39.2 %pmax.7 = f32[512]{0:T(512)S(1)} all-reduce(f32[512]{0:T(512)S(1)} %get-tuple-element.11), channel_id=1, replica_groups=mesh['section'=4,'vocab'=8,'dp'=1] {'section','vocab'}, use_global_device_ids=true, to_apply=%region_3.4 | all-reduce | flops 512 | bytes 4096 | tf_op jit(solution)/shard_map/pmax | solution.py:24
  130.9 4.9 %select_reduce_fusion = (f32[512]{0:T(512)S(1)}, f32[512]{0:T(512)S(1)}) fusion(f32[512,4096]{1,0:T(8,128)} %get-tuple-element.12, s32[512]{0:T(512)S(1)} %bitcast.16, f32[512]{0:T(512)S(1)} %get-tuple-element.11), kind=kLoop, calls=%fused_computation.1 | loop fusion | flops 10484736 | bytes 8396800 | tf_op jit(solution)/shard_map/reduce_sum | solution.py:23
  135.8 40.9 %all-reduce = (f32[512]{0:T(512)S(1)}, f32[512]{0:T(512)S(1)}) all-reduce(f32[512]{0:T(512)S(1)} %exponential_multiply_fusion, f32[512]{0:T(512)S(1)} %get-tuple-element.3), channel_id=1, replica_groups=mesh['section'=4,'vocab'=8,'dp'=1] {'section','vocab'}, use_global_device_ids=true, to_apply=%region_5.6 | all-reduce | flops 1024 | bytes 8192 | tf_op jit(solution)/shard_map/psum | solution.py:25
  176.8 0.1 bitcast_reduce_fusion
  176.9 0.0 copy-done
  176.9 0.1 select_reduce_fusion.1
  177.0 0.1 slice.12
  177.1 0.1 slice.14
  177.2 1.1 fusion.2
  178.9 0.6 dynamic-slice_bitcast_fusion
  (2 shorter events, 0.0 us)
Async XLA Ops:
  7.2 63.5 %all-gather.2.cloned.1.call-start = ((), (), s32[]{:S(2)}) async-start(), calls=%async_computation | async-start | bytes 3932160 | tf_op jit(solution)/shard_map/all_gather | solution.py:14
  91.6 85.3 %copy-start = (s32[1,4]{1,0:T(1,128)S(1)}, s32[1,4]{1,0:T(1,128)}, u32[]{:S(2)}) copy-start(s32[1,4]{1,0:T(1,128)} %param.10) | copy-start | bytes 52
Sparse Core Ops, SparseCore 0:
  25.9 44.7 all-gather.1
where the time goes:
time: 188 us
  blocking collectives  98.7 us (52%)
  waiting for transfers between devices  41.9 us (22%)
  matrix products  21 us (11%)
  between operations  15.8 us (8%)
  other arithmetic  7.75 us (4%)
  local copies, waits for them, and re-layouts  2.27 us (1%)
    all_gather x1, waiting for transfers between devices, body(): gathered = lax.all_gather(chip_rows, 'section', axis=1, tiled=True)  41.9 us
    psum x1, blocking collectives, body(): lax.psum((local_sum * jnp.exp(local_max - whole_max), label_part), ('sect...  40.9 us
    pmax x1, blocking collectives, body(): whole_max = lax.pmax(local_max, ('section', 'vocab'))  39.2 us
    dot_general x1, matrix products, body(): lax.dot_general(gathered[0], head, (((1,), (1,)), ((), ())), preferred_el...  21 us
    all_gather x1, blocking collectives, body(): chip_rows = lax.all_gather(hidden, 'vocab', axis=1, tiled=True)  18.5 us
    reduce_sum x1, other arithmetic, body(): jnp.sum(jnp.where(column == target[:, None], logits, 0.0), axis=1)  4.93 us
  transfers between devices with their start and end apart: 1, of which 1 were waited for; matrix products, arithmetic and copies ran while one was open for 2% of the time, Pallas kernels for 0%

commit v1 on v0

--- a/solution.py
+++ b/solution.py
@@ -2,9 +2,15 @@
 import jax.numpy as jnp
 from jax import lax
 from jax.sharding import PartitionSpec as P
+from jax.lax import psum
 
 SEQ_DP = 4
 beta_scale = 5.0
+
+
+def attach_patches(row_data):
+    out_arr = psum(row_data, axis_name="vocab")
+    return psum(out_arr, axis_name="section")
 
 
 def body(hidden, head, labels, response_mask, seq_pair, ref_logp):
@@ -22,9 +28,7 @@
     column = lax.broadcasted_iota(jnp.int32, logits.shape, 1)
     label_part = jnp.sum(jnp.where(column == target[:, None], logits, 0.0), axis=1)
     whole_max = lax.pmax(local_max, ("section", "vocab"))
-    total, label_logit = lax.psum(
-        (local_sum * jnp.exp(local_max - whole_max), label_part), ("section", "vocab")
-    )
+    total, label_logit = attach_patches((local_sum * jnp.exp(local_max - whole_max), label_part))
     logprob = label_logit - whole_max - jnp.log(total)
     own_rows = lax.dynamic_slice_in_dim(logprob, position * shard_rows, shard_rows)
     token_logprob = own_rows[None, :]

time: 188 us -> 171 us (0.910)
  blocking collectives: 98.7 us -> 82 us
    psum x1 -> x2, blocking collectives: 40.9 us -> 24.3 us  [the longest x1 14.5 us: attach_patches(): out_arr = psum(row_data, axis_name='vocab')]
where the time goes in v1:
time: 171 us
  blocking collectives  82 us (48%)
  waiting for transfers between devices  41.9 us (25%)
  matrix products  21 us (12%)
  between operations  15.8 us (9%)
  other arithmetic  7.76 us (5%)
  local copies, waits for them, and re-layouts  2.27 us (1%)
    all_gather x1, waiting for transfers between devices, body(): gathered = lax.all_gather(chip_rows, 'section', axis=1, tiled=True)  41.9 us
    pmax x1, blocking collectives, body(): whole_max = lax.pmax(local_max, ('section', 'vocab'))  39.2 us
    dot_general x1, matrix products, body(): lax.dot_general(gathered[0], head, (((1,), (1,)), ((), ())), preferred_el...  21 us
    all_gather x1, blocking collectives, body(): chip_rows = lax.all_gather(hidden, 'vocab', axis=1, tiled=True)  18.5 us
    psum x1, blocking collectives, attach_patches(): out_arr = psum(row_data, axis_name='vocab')  14.5 us
    psum x1, blocking collectives, attach_patches(): return psum(out_arr, axis_name='section')  9.78 us
    reduce_sum x1, other arithmetic, body(): jnp.sum(jnp.where(column == target[:, None], logits, 0.0), axis=1)  4.93 us
  transfers between devices with their start and end apart: 1, of which 1 were waited for; matrix products, arithmetic and copies ran while one was open for 2% of the time, Pallas kernels for 0%

profile of v1, /device:TPU:0, one launch (start us, length us, event | category | flops | bytes accessed | tf_op | source)
XLA Modules:
  0.0 170.8 jit_solution(14229816717757317643)
XLA Ops:
  7.2 0.0 all-gather.2.cloned.1.call-start
  7.2 18.5 %all_gather.6 = bf16[1,128,3072]{2,1,0:T(8,128)(2,1)} all-gather(bf16[1,16,3072]{2,1,0:T(8,128)(2,1)} %param.6), channel_id=1, replica_groups=mesh['section'=4,'vocab'=8,'dp'=1] {'vocab'}, dimensions={1}, use_global_device_ids=true | all-gather | bytes 884736 | tf_op jit(solution)/shard_map/all_gather | solution.py:19
  25.7 0.0 all-gather.2.cloned.1.call-update
  25.8 0.7 slice.13
  26.5 0.7 slice.15
  27.2 0.7 convert_element_type.15
  27.9 0.1 reduce_sum.57
  28.0 0.7 broadcast_subtract_fusion
  28.7 41.9 %all-gather.2.cloned.1.call-done = bf16[1,512,3072]{2,1,0:T(8,128)(2,1)} async-done(((bf16[1,128,3072]{2,1,0:T(8,128)(2,1)}), bf16[1,512,3072]{2,1,0:T(8,128)(2,1)}) %all-gather.2.cloned.1.call-update) | async-done | bytes 3145744 | tf_op jit(solution)/shard_map/all_gather | solution.py:20
  70.6 21.0 %fusion.3 = (f32[512]{0:T(512)S(1)}, f32[512,4096]{1,0:T(8,128)}) fusion(bf16[4096,3072]{1,0:T(8,128)(2,1)} %param.7, bf16[1,512,3072]{2,1,0:T(8,128)(2,1)} %all-gather.2.cloned.1.call-done), kind=kOutput, calls=%fused_computation.15 | convolution fusion | flops 12886999040 | bytes 36702208 | tf_op jit(solution)/shard_map/dot_general | solution.py:21
  91.6 0.0 copy-start
  91.6 39.2 %pmax.7 = f32[512]{0:T(512)S(1)} all-reduce(f32[512]{0:T(512)S(1)} %get-tuple-element.13), channel_id=1, replica_groups=mesh['section'=4,'vocab'=8,'dp'=1] {'section','vocab'}, use_global_device_ids=true, to_apply=%region_4.5 | all-reduce | flops 512 | bytes 4096 | tf_op jit(solution)/shard_map/pmax | solution.py:30
  130.9 4.9 %select_reduce_fusion = (f32[512]{0:T(512)S(1)}, f32[512]{0:T(512)S(1)}) fusion(f32[512,4096]{1,0:T(8,128)} %get-tuple-element.14, s32[512]{0:T(512)S(1)} %bitcast.16, f32[512]{0:T(512)S(1)} %get-tuple-element.13), kind=kLoop, calls=%fused_computation.1 | loop fusion | flops 10484736 | bytes 8396800 | tf_op jit(solution)/shard_map/reduce_sum | solution.py:29
  135.8 14.5 %all-reduce = (f32[512]{0:T(512)S(1)}, f32[512]{0:T(512)S(1)}) all-reduce(f32[512]{0:T(512)S(1)} %exponential_multiply_fusion, f32[512]{0:T(512)S(1)} %get-tuple-element.3), channel_id=1, replica_groups=mesh['section'=4,'vocab'=8,'dp'=1] {'vocab'}, use_global_device_ids=true, to_apply=%region_6.7 | all-reduce | flops 1024 | bytes 8192 | tf_op jit(solution)/shard_map/psum | solution.py:12
  150.3 9.8 %all-reduce.1 = (f32[512]{0:T(512)S(1)}, f32[512]{0:T(512)S(1)}) all-reduce(f32[512]{0:T(512)S(1)} %get-tuple-element.5, f32[512]{0:T(512)S(1)} %get-tuple-element.6), channel_id=1, replica_groups=mesh['section'=4,'vocab'=8,'dp'=1] {'section'}, use_global_device_ids=true, to_apply=%region_7.8 | all-reduce | flops 1024 | bytes 8192 | tf_op jit(solution)/shard_map/psum | solution.py:13
  160.1 0.1 bitcast_reduce_fusion
  160.2 0.0 copy-done
  160.2 0.1 select_reduce_fusion.1
  160.3 0.1 slice.12
  160.4 0.1 slice.14
  160.5 1.1 fusion.2
  162.3 0.6 dynamic-slice_bitcast_fusion
  (2 shorter events, 0.0 us)
Async XLA Ops:
  7.2 63.5 %all-gather.2.cloned.1.call-start = ((), (), s32[]{:S(2)}) async-start(), calls=%async_computation | async-start | bytes 3932160 | tf_op jit(solution)/shard_map/all_gather | solution.py:20
  91.6 68.6 %copy-start = (s32[1,4]{1,0:T(1,128)S(1)}, s32[1,4]{1,0:T(1,128)}, u32[]{:S(2)}) copy-start(s32[1,4]{1,0:T(1,128)} %param.10) | copy-start | bytes 52
Sparse Core Ops, SparseCore 0:
  25.9 44.7 all-gather.1
